TPU v7x, 512 devices: a whole 4x8x8 slice. The times are simulated.
512 devices in a mesh: req: 128 (over x, y_hi, z), row: 2 (over core), col: 2 (over y_lo).
Axes of the slice: x: 4, y: 8 (y_hi: 4, y_lo: 2; y = y_hi * 2 + y_lo), z: 8, core: 2. Of those that a mesh axis runs over, the one named last changes fastest.
Arguments:
- image_qkv: bfloat16 [3072, 24, 3, 1280], P(('req', 'row'), 'col'), parts along dimension 0, may hold values from -6 to 6
- text_kv: bfloat16 [12288, 2, 1280], P(('req', 'row'), None, 'col'), parts along dimension 0, may hold values from -6 to 6
- gain_query: float32 [64], replicated, may hold values from 1 to 3
- gain_key: float32 [64], replicated, may hold values from 1 to 3
- gain_text: float32 [64], replicated, may hold values from 1 to 3
- out_weight: bfloat16 [1280, 2432], P('col', 'row'), may hold values from -0.15625 to 0.15625
- final_weight: bfloat16 [64, 2432], P(None, 'row'), may hold values from -0.125 to 0.125
- hidden: bfloat16 [3072, 24, 2432], P(('req', 'row'), 'col'), parts along dimension 0, may hold values from -6 to 6
- modulation: float32 [384, 2432], P('req'), parts along dimension 0, may hold values from -3 to 3
- latent: float32 [6144, 768], P(('req', 'row'), 'col'), parts along dimension 0, may hold values from -6 to 6
- step_index: int32 [128], P('req'), parts along dimension 0, may hold values from 0 to 20
- step_count: int32 [128], P('req'), parts along dimension 0, may hold values from 1 to 5
Outputs:
- velocity: float32 [6144, 768], P(('req', 'row'), 'col'), parts along dimension 0
- latent_next: float32 [6144, 768], P(('req', 'row'), 'col'), parts along dimension 0
There are 128 independent parts, one for each index of `req`. A program takes and returns all parts, laid end to end along the dimension named above; an argument that names none is the same for every part. Nothing has to cross between parts.
All inputs are finite; a program needn't handle non-finite values.
Results may differ from a plain program's by a relative error of at most 0.009.
Values may be sent and summed in bfloat16 or wider, within the bound.
A program may use at most 128 MiB of HBM per device.

v0:
```python
import jax
import jax.numpy as jnp
from jax import lax
from jax.experimental import pallas as pl
from jax.experimental.pallas import tpu as pltpu
from jax.sharding import PartitionSpec as P

HEAD = 64
CH = 16
PATCH = 2
STEPS = 28
SHIFT_FACTOR = 3.0
EPS = 1e-06
LANES = 128
MESH = pl.DeviceIdType.MESH
F32, BF16 = jnp.float32, jnp.bfloat16


def noise_level(step_number):
    fraction = 1.0 - step_number.astype(F32) / STEPS
    return SHIFT_FACTOR * fraction / (1.0 + (SHIFT_FACTOR - 1.0) * fraction)


def block_kernel(
    qkv_hbm, text_hbm, gq_ref, gk_ref, gt_ref, wt_hbm, fw_hbm, hid_hbm, mod_hbm,
    vel_ref,
    qkv, text, hid_in, hid, mod, fw, fw_full, gains, block,
    v_out, k_out, q_out, q_own, q_peer, k_all, v_all, w_all,
    p_out, p_own, p_in,
    load_sem, send_sem, recv_sem, q_send, q_recv, p_send, p_recv,
):
    row, col = lax.axis_index("row"), lax.axis_index("col")
    to_row, to_col = {"row": 1 - row}, {"col": 1 - col}
    tile = qkv.shape[0]
    words = text.shape[0]
    width = k_all.shape[1]
    half = wt_hbm.shape[0]
    features = w_all.shape[0]
    chunk = q_send.shape[0]
    rows = tile // chunk
    pairs = width // LANES

    def load(source, target, at):
        return pltpu.make_async_copy(source, target, load_sem.at[at])

    def remote(source, target, at, device):
        return pltpu.make_async_remote_copy(
            src_ref=source, dst_ref=target, send_sem=send_sem.at[at], recv_sem=recv_sem.at[at],
            device_id=device, device_id_type=MESH,
        )

    own_half = pl.ds(pl.multiple_of(row * half, 64), half)
    load_qkv = load(qkv_hbm, qkv, 0)
    load_text = load(text_hbm, text, 1)
    load_w = load(wt_hbm, w_all.at[own_half], 2)
    load_fw = load(fw_hbm, fw.at[row], 3)
    load_hid = load(hid_hbm, hid_in, 4)
    load_mod = load(mod_hbm, mod, 5)
    load_qkv.start()
    load_text.start()
    load_w.start()
    load_fw.start()
    load_hid.start()
    load_mod.start()

    barrier = pltpu.get_barrier_semaphore()
    pl.semaphore_signal(barrier, inc=1, device_id=to_row, device_id_type=MESH)
    pl.semaphore_signal(barrier, inc=1, device_id=to_col, device_id_type=MESH)

    for at, ref in enumerate((gq_ref, gk_ref, gt_ref)):
        gains[at : at + 1, 0:HEAD] = ref[...]
        gains[at : at + 1, HEAD:LANES] = ref[...]
    down = lax.broadcasted_iota(jnp.int32, (2 * LANES, LANES), 0) // HEAD
    across = lax.broadcasted_iota(jnp.int32, (2 * LANES, LANES), 1) // HEAD
    block[...] = jnp.where(down % 2 == across, 1.0 / HEAD, 0.0).astype(BF16)

    pl.semaphore_wait(barrier, 2)

    w_copy = remote(wt_hbm, w_all.at[own_half], 0, to_row)
    fw_copy = remote(fw_hbm, fw.at[row], 1, to_row)

    def head_norm(values, gain):
        count = values.shape[0]
        pieces = [values[:, LANES * at : LANES * (at + 1)] for at in range(pairs)]
        stacked = jnp.concatenate(pieces, axis=0).astype(F32)
        square = stacked * stacked
        high = square.astype(BF16)
        low = (square - high.astype(F32)).astype(BF16)
        mean = jnp.dot(
            jnp.concatenate([high, low], axis=1), block[...], preferred_element_type=F32
        )
        normed = (stacked * lax.rsqrt(mean + EPS) * gain).astype(BF16)
        return jnp.concatenate(
            [normed[count * at : count * (at + 1)] for at in range(pairs)], axis=1
        )

    mine = pl.ds(pl.multiple_of(col * width, LANES), width)
    other = pl.ds(pl.multiple_of((1 - col) * width, LANES), width)
    own_rows, col_rows = pl.ds(0, tile), pl.ds(tile, tile)
    row_rows, far_rows = pl.ds(2 * tile, tile), pl.ds(3 * tile, tile)
    own_text, row_text = pl.ds(4 * tile, words), pl.ds(4 * tile + words, words)

    load_qkv.wait()
    v_out[...] = qkv[:, 2, other]
    v_col = remote(v_out, v_all.at[col_rows], 2, to_col)
    v_col.start()
    k_out[...] = head_norm(qkv[:, 1, other], gains[1:2])
    k_col = remote(k_out, k_all.at[col_rows], 3, to_col)
    k_col.start()
    w_copy.start()
    fw_copy.start()
    q_out[...] = head_norm(qkv[:, 0, other], gains[0:1] * 0.125)

    def q_copy(at):
        part = pl.ds(pl.multiple_of(at * rows, 16), rows)
        return pltpu.make_async_remote_copy(
            src_ref=q_out.at[part], dst_ref=q_peer.at[part],
            send_sem=q_send.at[at], recv_sem=q_recv.at[at],
            device_id=to_col, device_id_type=MESH,
        )

    for at in range(chunk):
        q_copy(at).start()

    v_all[own_rows, :] = qkv[:, 2, mine]
    v_row = remote(v_all.at[own_rows], v_all.at[row_rows], 4, to_row)
    v_row.start()
    k_all[own_rows, :] = head_norm(qkv[:, 1, mine], gains[1:2])
    k_row = remote(k_all.at[own_rows], k_all.at[row_rows], 5, to_row)
    k_row.start()
    load_text.wait()
    v_all[own_text, :] = text[:, 1, :]
    vt_row = remote(v_all.at[own_text], v_all.at[row_text], 6, to_row)
    vt_row.start()
    k_all[own_text, :] = head_norm(text[:, 0, :], gains[2:3])
    kt_row = remote(k_all.at[own_text], k_all.at[row_text], 7, to_row)
    kt_row.start()
    q_own[...] = head_norm(qkv[:, 0, mine], gains[0:1] * 0.125)

    load_hid.wait()
    grid_cols = hid_in.shape[1]
    for at in range(hid_in.shape[0]):
        hid[grid_cols * at : grid_cols * (at + 1), :] = hid_in[at]

    v_col.wait_recv()
    v_far = remote(v_all.at[col_rows], v_all.at[far_rows], 8, to_row)
    v_far.start()
    load_fw.wait()
    fw_copy.wait()
    fw_full[:, 0:half] = fw[0]
    fw_full[:, half:features] = fw[1]
    k_col.wait_recv()
    k_far = remote(k_all.at[col_rows], k_all.at[far_rows], 9, to_row)
    k_far.start()
    load_w.wait()
    w_copy.wait()
    load_mod.wait()
    v_row.wait()
    k_row.wait()
    vt_row.wait()
    kt_row.wait()
    v_far.wait()
    k_far.wait()

    low_half = lax.broadcasted_iota(jnp.int32, (rows, LANES), 1) < HEAD
    ones = jnp.ones((k_all.shape[0], LANES), BF16)

    def attend(queries):
        parts = []
        for at in range(pairs):
            lanes = slice(LANES * at, LANES * (at + 1))
            pair = queries[:, lanes].astype(F32)
            both = jnp.concatenate(
                [jnp.where(low_half, pair, 0.0), jnp.where(low_half, 0.0, pair)], axis=0
            ).astype(BF16)
            scores = lax.dot_general(
                both, k_all[:, lanes], (((1,), (1,)), ((), ())), preferred_element_type=F32
            )
            weights = jnp.exp(scores).astype(BF16)
            sums = jnp.dot(
                weights, jnp.concatenate([v_all[:, lanes], ones], axis=1),
                preferred_element_type=F32,
            )
            weighted = jnp.where(low_half, sums[:rows, :LANES], sums[rows:, :LANES])
            totals = jnp.where(low_half, sums[:rows, LANES:], sums[rows:, LANES:])
            parts.append((weighted / totals).astype(BF16))
        return jnp.concatenate(parts, axis=1)

    def project(attended):
        return lax.dot_general(
            attended, w_all[...], (((1,), (1,)), ((), ())), preferred_element_type=F32
        ).astype(BF16)

    def p_copy(at):
        part = pl.ds(pl.multiple_of(at * rows, 16), rows)
        return pltpu.make_async_remote_copy(
            src_ref=p_out.at[part], dst_ref=p_in.at[part],
            send_sem=p_send.at[at], recv_sem=p_recv.at[at],
            device_id=to_col, device_id_type=MESH,
        )

    @pl.loop(0, chunk)
    def _(at):
        part = pl.ds(pl.multiple_of(at * rows, 16), rows)
        q_copy(at).wait_recv()
        p_out[part, :] = project(attend(q_peer[part, :]))
        p_copy(at).start()

    @pl.loop(0, chunk)
    def _(at):
        part = pl.ds(pl.multiple_of(at * rows, 16), rows)
        p_own[part, :] = project(attend(q_own[part, :]))

    @pl.loop(0, chunk)
    def _(at):
        part = pl.ds(pl.multiple_of(at * rows, 16), rows)
        p_copy(at).wait_recv()
        projected = p_own[part, :].astype(F32) + p_in[part, :].astype(F32)
        mixed = hid[part, :].astype(F32) + mod[2:3, :] * projected
        mean = jnp.sum(mixed, axis=-1, keepdims=True) * (1.0 / features)
        centered = mixed - mean
        var = jnp.sum(centered * centered, axis=-1, keepdims=True) * (1.0 / features)
        normed = centered * lax.rsqrt(var + EPS) * (1.0 + mod[1:2, :]) + mod[0:1, :]
        vel_ref[part, :] = lax.dot_general(
            normed.astype(BF16), fw_full[...], (((1,), (1,)), ((), ())),
            preferred_element_type=F32,
        )

    v_col.wait_send()
    k_col.wait_send()

    @pl.loop(0, chunk)
    def _(at):
        q_copy(at).wait_send()
        p_copy(at).wait_send()


def on_device(
    image_qkv, text_kv, gain_query, gain_key, gain_text, out_weight, final_weight,
    hidden, modulation, latent, step_index, step_count,
):
    tile_rows, tile_cols, _, heads_width = image_qkv.shape
    tile = tile_rows * tile_cols
    words, _, width = text_kv.shape
    half = out_weight.shape[1]
    features = hidden.shape[2]
    patch_values = final_weight.shape[0]
    keys = 4 * tile + 2 * words
    chunk = 3
    anywhere = pl.BlockSpec(memory_space=pl.ANY)
    vmem = pl.BlockSpec(memory_space=pltpu.VMEM)
    velocity = pl.pallas_call(
        block_kernel,
        out_shape=jax.ShapeDtypeStruct((tile, patch_values), F32),
        in_specs=[anywhere, anywhere, vmem, vmem, vmem, anywhere, anywhere, anywhere, anywhere],
        out_specs=vmem,
        scratch_shapes=[
            pltpu.VMEM((tile, 3, heads_width), BF16),
            pltpu.VMEM((words, 2, width), BF16),
            pltpu.VMEM((tile_rows, tile_cols, features), BF16),
            pltpu.VMEM((tile, features), BF16),
            pltpu.VMEM((3, features), F32),
            pltpu.VMEM((2, patch_values, half), BF16),
            pltpu.VMEM((patch_values, features), BF16),
            pltpu.VMEM((8, LANES), F32),
            pltpu.VMEM((2 * LANES, LANES), BF16),
            pltpu.VMEM((tile, width), BF16),
            pltpu.VMEM((tile, width), BF16),
            pltpu.VMEM((tile, width), BF16),
            pltpu.VMEM((tile, width), BF16),
            pltpu.VMEM((tile, width), BF16),
            pltpu.VMEM((keys, width), BF16),
            pltpu.VMEM((keys, width), BF16),
            pltpu.VMEM((features, width), BF16),
            pltpu.VMEM((tile, features), BF16),
            pltpu.VMEM((tile, features), BF16),
            pltpu.VMEM((tile, features), BF16),
            pltpu.SemaphoreType.DMA((6,)),
            pltpu.SemaphoreType.DMA((10,)),
            pltpu.SemaphoreType.DMA((10,)),
            pltpu.SemaphoreType.DMA((chunk,)),
            pltpu.SemaphoreType.DMA((chunk,)),
            pltpu.SemaphoreType.DMA((chunk,)),
            pltpu.SemaphoreType.DMA((chunk,)),
        ],
        compiler_params=pltpu.CompilerParams(
            collective_id=0, has_side_effects=True
        ),
        name="attention_block",
    )(
        image_qkv.reshape(tile, 3, heads_width), text_kv,
        gain_query.reshape(1, HEAD), gain_key.reshape(1, HEAD), gain_text.reshape(1, HEAD),
        out_weight.T, final_weight, hidden, modulation,
    )
    velocity = (
        velocity.reshape(tile_rows, tile_cols, PATCH, PATCH, CH)
        .transpose(0, 2, 1, 3, 4)
        .reshape(tile_rows * PATCH, tile_cols * PATCH * CH)
    )
    euler_step = noise_level(step_index[0] + step_count[0]) - noise_level(step_index[0])
    return (velocity, latent + euler_step * velocity)


def solution(mesh):
    placed = (
        P(("req", "row"), "col", None, None),
        P(("req", "row"), None, "col"),
        P(),
        P(),
        P(),
        P("col", "row"),
        P(None, "row"),
        P(("req", "row"), "col", None),
        P("req", None),
        P(("req", "row"), "col"),
        P("req"),
        P("req"),
    )
    return jax.shard_map(
        on_device,
        mesh=mesh,
        in_specs=placed,
        out_specs=(P(("req", "row"), "col"), P(("req", "row"), "col")),
        check_vma=False,
    )
```

profile of v0, /device:TPU:1, one launch (start us, length us, event | category | flops | bytes accessed | tf_op | source)
XLA Modules:
  0.0 46.1 jit_solution(4615828415504034194)
XLA Ops:
  0.6 0.0 copy-start.1
  0.6 41.8 %attention_block.1 = f32[144,64]{1,0:T(8,128)} custom-call(bf16[144,3,1280]{2,1,0:T(4,128)(2,1)} %bitcast.8, bf16[48,2,640]{2,1,0:T(2,128)(2,1)} %text_hbm.1, f32[1,64]{1,0:T(1,128)} %bitcast.10, f32[1,64]{1,0:T(1,128)} %bitcast.11, f32[1,64]{1,0:T(1,128)} %bitcast.12, bf16[1216,640]{1,0:T(8,128)(2,1)} %bitcast.7, bf16[64,1216]{1,0:T(8,128)(2,1)} %fw_hbm.1, ...), custom_call_target="tpu_custom_call" | custom-call | tf_op jit(solution)/shard_map/attention_block/pallas_call | solution.py:252
  42.4 1.1 %reshape.41 = f32[12,12,2,2,16]{4,3,2,1,0:T(2,128)S(1)} reshape(f32[144,64]{1,0:T(8,128)} %attention_block.1) | data formatting | bytes 73728 | tf_op jit(solution)/shard_map/reshape | solution.py:296
  43.6 0.1 copy.15
  43.7 0.4 reshape.42
  44.0 0.0 copy-start
  45.5 0.0 copy-done.1
  45.5 0.6 %multiply_add_fusion = f32[24,384]{1,0:T(8,128)} fusion(f32[24,384]{1,0:T(8,128)S(1)} %copy-done.1, f32[24,384]{1,0:T(8,128)S(1)} %reshape.42, f32[]{:T(128)} %bitcast.6), kind=kLoop, calls=%fused_computation | loop fusion | flops 18432 | bytes 110596 | tf_op jit(solution)/shard_map/add | solution.py:301
  46.1 0.0 copy-done
Async XLA Ops:
  0.6 44.8 %copy-start.1 = (f32[24,384]{1,0:T(8,128)S(1)}, f32[24,384]{1,0:T(8,128)}, u32[]{:S(2)}) copy-start(f32[24,384]{1,0:T(8,128)} %param.21) | copy-start | bytes 110596
  44.0 2.0 %copy-start = (f32[24,384]{1,0:T(8,128)}, f32[24,384]{1,0:T(8,128)S(1)}, u32[]{:S(2)}) copy-start(f32[24,384]{1,0:T(8,128)S(1)} %reshape.42) | copy-start | bytes 110596
where the time goes:
time: 46.3 us; the launch traced here: 46.1 us
  Pallas kernels  41.8 us (90%)
  between operations  2.08 us (4%)
  local copies, waits for them, and re-layouts  1.62 us (3%)
  other arithmetic  0.62 us (1%)
    pallas_call x1, Pallas kernels, on_device(): pl.pallas_call(block_kernel, out_shape=jax.ShapeDtypeStruct((tile, patch_...  41.8 us
    reshape x1, local copies, waits for them, and re-layouts, on_device(): velocity.reshape(tile_rows, tile_cols, PATCH, PATCH, CH)  1.15 us

commit v1 on v0

v1 whole, which is shorter than its diff:
```python
import functools

import jax
import jax.numpy as jnp
from jax import lax
from jax.experimental import pallas as pl
from jax.experimental.pallas import tpu as pltpu
from jax.sharding import PartitionSpec as P

HEAD = 64
CH = 16
PATCH = 2
STEPS = 28
SHIFT_FACTOR = 3.0
EPS = 1e-06
LANES = 128
TORUS = (4, 4, 8)
MESH = pl.DeviceIdType.MESH
F32, BF16 = jnp.float32, jnp.bfloat16


def noise_level(step_number):
    fraction = 1.0 - step_number.astype(F32) / STEPS
    return SHIFT_FACTOR * fraction / (1.0 + (SHIFT_FACTOR - 1.0) * fraction)


def block_kernel(
    torus,
    qkv_hbm, text_hbm, gq_ref, gk_ref, gt_ref, wt_hbm, fw_hbm, hid_hbm, mod_hbm,
    vel_ref,
    qkv, text, hid_in, hid, mod, fw, fw_full, gains, block,
    v_out, k_out, q_out, q_all, k_all, v_all, w_own, w_oth,
    att_out, att_in, att_own, p_own, p_oth,
    load_sem, send_sem, recv_sem, pair_send, pair_recv, w_send, w_recv,
):
    row, col = lax.axis_index("row"), lax.axis_index("col")
    to_row, to_col = {"row": 1 - row}, {"col": 1 - col}
    tile = qkv.shape[0]
    words = text.shape[0]
    pairs, keys, _ = k_all.shape
    width = pairs * LANES
    half = wt_hbm.shape[0]
    features = w_own.shape[0]

    def load(source, target, at):
        return pltpu.make_async_copy(source, target, load_sem.at[at])

    def remote(source, target, sems, at, device):
        return pltpu.make_async_remote_copy(
            src_ref=source, dst_ref=target, send_sem=sems[0].at[at], recv_sem=sems[1].at[at],
            device_id=device, device_id_type=MESH,
        )

    plain, paired, weight = (send_sem, recv_sem), (pair_send, pair_recv), (w_send, w_recv)

    own_half = pl.ds(pl.multiple_of(row * half, 64), half)
    load_qkv = load(qkv_hbm, qkv, 0)
    load_text = load(text_hbm, text, 1)
    load_w = load(wt_hbm, w_own.at[own_half], 2)
    load_fw = load(fw_hbm, fw.at[row], 3)
    load_hid = load(hid_hbm, hid_in, 4)
    load_mod = load(mod_hbm, mod, 5)
    load_qkv.start()
    load_text.start()
    load_w.start()
    load_fw.start()
    load_hid.start()
    load_mod.start()

    partners = [to_row, to_col]
    if torus:
        size_x, size_y, size_z = torus
        req = lax.axis_index("req")
        at_z = req % size_z
        at_y = (req // size_z) % size_y
        at_x = req // (size_z * size_y)

        def chip(x, y, z):
            return ((x % size_x) * size_y + y % size_y) * size_z + z % size_z

        to_y = {"req": chip(at_x, at_y + size_y + 2 * col - 1, at_z), "col": 1 - col}
        to_x = [{"req": chip(at_x + step, at_y, at_z)} for step in (1, size_x - 1)]
        to_z = [{"req": chip(at_x, at_y, at_z + step)} for step in (1, size_z - 1)]
        partners += [to_y, *to_x, *to_z]

    barrier = pltpu.get_barrier_semaphore()
    for partner in partners:
        pl.semaphore_signal(barrier, inc=1, device_id=partner, device_id_type=MESH)

    for at, ref in enumerate((gq_ref, gk_ref, gt_ref)):
        gains[at : at + 1, 0:HEAD] = ref[...]
        gains[at : at + 1, HEAD:LANES] = ref[...]
    down = lax.broadcasted_iota(jnp.int32, (2 * LANES, LANES), 0) // HEAD
    across = lax.broadcasted_iota(jnp.int32, (2 * LANES, LANES), 1) // HEAD
    block[...] = jnp.where(down % 2 == across, 1.0 / HEAD, 0.0).astype(BF16)

    pl.semaphore_wait(barrier, len(partners))

    if torus:
        quarter = half // 4
        first = quarter // 32 * 16 + 16
        parts = ((0, first), (first, quarter - first))
        colour = (at_x + 2 * at_z) % 4

        def piece(which, part, base):
            start, count = parts[part]
            offset = base + (which % 4) * quarter + start
            return pl.ds(pl.multiple_of(offset, 16), count)

        def near(part):
            return remote(
                wt_hbm.at[piece(colour, part, 0)],
                w_oth.at[piece(colour, part, row * half)], weight, part, to_y,
            )

        def spread(which, part, at, device):
            rows = piece(which, part, row * half)
            return remote(w_oth.at[rows], w_oth.at[rows], weight, at, device)

        def across_x(part, side, which):
            return spread(which, part, 2 + 2 * side + part, to_x[side])

        def across_z(part, which):
            return spread(which, part, 6 + part, to_z[part])

        def across_row(which, part, at):
            return spread(which, part, at, to_row)

        near(0).start()
        near(1).start()
    else:
        near = remote(wt_hbm, w_oth.at[own_half], weight, 0, to_col)
    w_row = remote(wt_hbm, w_own.at[own_half], plain, 0, to_row)
    fw_row = remote(fw_hbm, fw.at[row], plain, 1, to_row)

    def head_norm(values, gain):
        count = values.shape[0]
        pieces = [values[:, LANES * at : LANES * (at + 1)] for at in range(pairs)]
        stacked = jnp.concatenate(pieces, axis=0).astype(F32)
        square = stacked * stacked
        high = square.astype(BF16)
        low = (square - high.astype(F32)).astype(BF16)
        mean = jnp.dot(
            jnp.concatenate([high, low], axis=1), block[...], preferred_element_type=F32
        )
        normed = (stacked * lax.rsqrt(mean + EPS) * gain).astype(BF16)
        return normed.reshape(pairs, count, LANES)

    def split(values):
        return [values[:, LANES * at : LANES * (at + 1)] for at in range(pairs)]

    mine = pl.ds(pl.multiple_of(col * width, LANES), width)
    other = pl.ds(pl.multiple_of((1 - col) * width, LANES), width)
    own_rows, col_rows = pl.ds(0, tile), pl.ds(tile, tile)
    row_rows, far_rows = pl.ds(2 * tile, tile), pl.ds(3 * tile, tile)
    own_text, row_text = pl.ds(4 * tile, words), pl.ds(4 * tile + words, words)

    def k_col(at):
        return remote(k_out.at[at], k_all.at[at, col_rows], paired, at, to_col)

    def v_col(at):
        return remote(v_out.at[at], v_all.at[at, col_rows], paired, pairs + at, to_col)

    def q_col(at):
        return remote(q_out.at[at], q_all.at[at, own_rows], paired, 2 * pairs + at, to_col)

    def k_far(at):
        return remote(
            k_all.at[at, col_rows], k_all.at[at, far_rows], paired, 3 * pairs + at, to_row
        )

    def v_far(at):
        return remote(
            v_all.at[at, col_rows], v_all.at[at, far_rows], paired, 4 * pairs + at, to_row
        )

    def att_col(at):
        return remote(att_out.at[at], att_in.at[at], paired, 5 * pairs + at, to_col)

    load_qkv.wait()
    for at, part in enumerate(split(qkv[:, 2, other])):
        v_out[at] = part
    v_col(0).start()
    v_col(1).start()
    k_out[...] = head_norm(qkv[:, 1, other], gains[1:2])
    k_col(0).start()
    q_out[...] = head_norm(qkv[:, 0, other], gains[0:1] * 0.125)
    q_col(0).start()
    k_col(1).start()
    q_col(1).start()
    for at in range(2, pairs):
        k_col(at).start()
        v_col(at).start()
        q_col(at).start()

    for at, part in enumerate(split(qkv[:, 2, mine])):
        v_all[at, own_rows, :] = part
    v_row = remote(v_all.at[:, own_rows], v_all.at[:, row_rows], plain, 2, to_row)
    v_row.start()
    k_all[:, own_rows, :] = head_norm(qkv[:, 1, mine], gains[1:2])
    k_row = remote(k_all.at[:, own_rows], k_all.at[:, row_rows], plain, 3, to_row)
    k_row.start()
    load_text.wait()
    for at, part in enumerate(split(text[:, 1, :])):
        v_all[at, own_text, :] = part
    vt_row = remote(v_all.at[:, own_text], v_all.at[:, row_text], plain, 4, to_row)
    vt_row.start()
    k_all[:, own_text, :] = head_norm(text[:, 0, :], gains[2:3])
    kt_row = remote(k_all.at[:, own_text], k_all.at[:, row_text], plain, 5, to_row)
    kt_row.start()
    w_row.start()
    fw_row.start()
    if not torus:
        near.start()
    q_all[:, col_rows, :] = head_norm(qkv[:, 0, mine], gains[0:1] * 0.125)

    def spread_near(part):
        near(part).wait_recv()
        across_x(part, 0, colour).start()
        across_x(part, 1, colour).start()
        across_z(part, colour).start()
        across_row(colour, part, 8 + part).start()

    v_row.wait()
    k_row.wait()
    vt_row.wait()
    kt_row.wait()

    low_half = lax.broadcasted_iota(jnp.int32, (tile, LANES), 1) < HEAD
    ones = jnp.ones((keys, LANES), BF16)

    def attend(at, rows):
        pair = q_all[at, rows, :].astype(F32)
        both = jnp.concatenate(
            [jnp.where(low_half, pair, 0.0), jnp.where(low_half, 0.0, pair)], axis=0
        ).astype(BF16)
        scores = lax.dot_general(
            both, k_all[at], (((1,), (1,)), ((), ())), preferred_element_type=F32
        )
        weights = jnp.exp(scores).astype(BF16)
        sums = jnp.dot(
            weights, jnp.concatenate([v_all[at], ones], axis=1), preferred_element_type=F32
        )
        weighted = jnp.where(low_half, sums[:tile, :LANES], sums[tile:, :LANES])
        totals = jnp.where(low_half, sums[:tile, LANES:], sums[tile:, LANES:])
        return (weighted / totals).astype(BF16)

    def attend_pair(at):
        k_far(at).wait_recv()
        v_far(at).wait_recv()
        q_col(at).wait_recv()
        att_out[at] = attend(at, own_rows)
        att_col(at).start()
        att_own[at] = attend(at, col_rows)

    grid_cols = hid_in.shape[1]
    for at in range(pairs):
        k_col(at).wait_recv()
        k_far(at).start()
        v_col(at).wait_recv()
        v_far(at).start()
        if at == 0:
            load_hid.wait()
            for line in range(hid_in.shape[0]):
                hid[grid_cols * line : grid_cols * (line + 1), :] = hid_in[line]
        else:
            attend_pair(at - 1)
        if torus and at == 0:
            spread_near(0)
        if torus and at == 1:
            spread_near(1)
        if torus and at == pairs - 1:
            for part in range(2):
                across_x(part, 0, colour + 3).wait_recv()
                across_row(colour + 3, part, 10 + part).start()
                across_x(part, 1, colour + 1).wait_recv()
                across_row(colour + 1, part, 12 + part).start()
                across_z(part, colour + 2).wait_recv()
                across_row(colour + 2, part, 14 + part).start()
        if at == 1:
            load_fw.wait()
            fw_row.wait()
            fw_full[:, 0:half] = fw[0]
            fw_full[:, half:features] = fw[1]
    attend_pair(pairs - 1)

    def project(attended, weights):
        joined = jnp.concatenate([attended[at] for at in range(pairs)], axis=1)
        return lax.dot_general(
            joined, weights[...], (((1,), (1,)), ((), ())), preferred_element_type=F32
        ).astype(BF16)

    load_w.wait()
    w_row.wait()
    p_own[...] = project(att_own, w_own)
    if torus:
        for part in range(2):
            across_row(colour, part, 8 + part).wait()
            across_row(colour + 3, part, 10 + part).wait()
            across_row(colour + 1, part, 12 + part).wait()
            across_row(colour + 2, part, 14 + part).wait()
    else:
        near.wait()
        w_far = remote(w_oth.at[own_half], w_oth.at[own_half], weight, 1, to_row)
        w_far.start()
        w_far.wait()
    for at in range(pairs):
        att_col(at).wait_recv()
    p_oth[...] = project(att_in, w_oth)
    load_mod.wait()

    rows = tile // 3

    @pl.loop(0, 3)
    def _(at):
        part = pl.ds(pl.multiple_of(at * rows, 16), rows)
        projected = p_own[part, :].astype(F32) + p_oth[part, :].astype(F32)
        mixed = hid[part, :].astype(F32) + mod[2:3, :] * projected
        mean = jnp.sum(mixed, axis=-1, keepdims=True) * (1.0 / features)
        centered = mixed - mean
        var = jnp.sum(centered * centered, axis=-1, keepdims=True) * (1.0 / features)
        normed = centered * lax.rsqrt(var + EPS) * (1.0 + mod[1:2, :]) + mod[0:1, :]
        vel_ref[part, :] = lax.dot_general(
            normed.astype(BF16), fw_full[...], (((1,), (1,)), ((), ())),
            preferred_element_type=F32,
        )

    for at in range(pairs):
        for copy in (k_col, v_col, q_col, k_far, v_far, att_col):
            copy(at).wait_send()
    if torus:
        for part in range(2):
            near(part).wait_send()
            across_x(part, 0, colour).wait_send()
            across_x(part, 1, colour).wait_send()
            across_z(part, colour).wait_send()


def on_device(
    torus,
    image_qkv, text_kv, gain_query, gain_key, gain_text, out_weight, final_weight,
    hidden, modulation, latent, step_index, step_count,
):
    tile_rows, tile_cols, _, heads_width = image_qkv.shape
    tile = tile_rows * tile_cols
    words, _, width = text_kv.shape
    half = out_weight.shape[1]
    features = hidden.shape[2]
    patch_values = final_weight.shape[0]
    keys = 4 * tile + 2 * words
    pairs = width // LANES
    anywhere = pl.BlockSpec(memory_space=pl.ANY)
    vmem = pl.BlockSpec(memory_space=pltpu.VMEM)
    velocity = pl.pallas_call(
        functools.partial(block_kernel, torus),
        out_shape=jax.ShapeDtypeStruct((tile, patch_values), F32),
        in_specs=[anywhere, anywhere, vmem, vmem, vmem, anywhere, anywhere, anywhere, anywhere],
        out_specs=vmem,
        scratch_shapes=[
            pltpu.VMEM((tile, 3, heads_width), BF16),
            pltpu.VMEM((words, 2, width), BF16),
            pltpu.VMEM((tile_rows, tile_cols, features), BF16),
            pltpu.VMEM((tile, features), BF16),
            pltpu.VMEM((3, features), F32),
            pltpu.VMEM((2, patch_values, half), BF16),
            pltpu.VMEM((patch_values, features), BF16),
            pltpu.VMEM((8, LANES), F32),
            pltpu.VMEM((2 * LANES, LANES), BF16),
            pltpu.VMEM((pairs, tile, LANES), BF16),
            pltpu.VMEM((pairs, tile, LANES), BF16),
            pltpu.VMEM((pairs, tile, LANES), BF16),
            pltpu.VMEM((pairs, 2 * tile, LANES), BF16),
            pltpu.VMEM((pairs, keys, LANES), BF16),
            pltpu.VMEM((pairs, keys, LANES), BF16),
            pltpu.VMEM((features, width), BF16),
            pltpu.VMEM((features, width), BF16),
            pltpu.VMEM((pairs, tile, LANES), BF16),
            pltpu.VMEM((pairs, tile, LANES), BF16),
            pltpu.VMEM((pairs, tile, LANES), BF16),
            pltpu.VMEM((tile, features), BF16),
            pltpu.VMEM((tile, features), BF16),
            pltpu.SemaphoreType.DMA((6,)),
            pltpu.SemaphoreType.DMA((6,)),
            pltpu.SemaphoreType.DMA((6,)),
            pltpu.SemaphoreType.DMA((6 * pairs,)),
            pltpu.SemaphoreType.DMA((6 * pairs,)),
            pltpu.SemaphoreType.DMA((16,)),
            pltpu.SemaphoreType.DMA((16,)),
        ],
        compiler_params=pltpu.CompilerParams(collective_id=0, has_side_effects=True),
        name="attention_block",
    )(
        image_qkv.reshape(tile, 3, heads_width), text_kv,
        gain_query.reshape(1, HEAD), gain_key.reshape(1, HEAD), gain_text.reshape(1, HEAD),
        out_weight.T, final_weight, hidden, modulation,
    )
    velocity = (
        velocity.reshape(tile_rows, tile_cols, PATCH, PATCH, CH)
        .transpose(0, 2, 1, 3, 4)
        .reshape(tile_rows * PATCH, tile_cols * PATCH * CH)
    )
    euler_step = noise_level(step_index[0] + step_count[0]) - noise_level(step_index[0])
    return (velocity, latent + euler_step * velocity)


def solution(mesh):
    placed = (
        P(("req", "row"), "col", None, None),
        P(("req", "row"), None, "col"),
        P(),
        P(),
        P(),
        P("col", "row"),
        P(None, "row"),
        P(("req", "row"), "col", None),
        P("req", None),
        P(("req", "row"), "col"),
        P("req"),
        P("req"),
    )
    torus = TORUS if mesh.shape["req"] == TORUS[0] * TORUS[1] * TORUS[2] else None
    return jax.shard_map(
        functools.partial(on_device, torus),
        mesh=mesh,
        in_specs=placed,
        out_specs=(P(("req", "row"), "col"), P(("req", "row"), "col")),
        check_vma=False,
    )
```

time: 46.3 us -> 42.9 us (0.927)
  Pallas kernels: 41.8 us -> 38 us
    pallas_call x1, Pallas kernels: 41.8 us -> 38 us  [on_device(): pl.pallas_call(functools.partial(block_kernel, torus), out_shape=jax.Shap...]
where the time goes in v1:
time: 42.9 us; the launch traced here: 42.3 us
  Pallas kernels  38 us (89%)
  between operations  2.08 us (5%)
  local copies, waits for them, and re-layouts  1.62 us (4%)
  other arithmetic  0.62 us (1%)
    pallas_call x1, Pallas kernels, on_device(): pl.pallas_call(functools.partial(block_kernel, torus), out_shape=jax.Shap...  38 us
    reshape x1, local copies, waits for them, and re-layouts, on_device(): velocity.reshape(tile_rows, tile_cols, PATCH, PATCH, CH)  1.15 us

profile of v1, /device:TPU:1, one launch (start us, length us, event | category | flops | bytes accessed | tf_op | source)
XLA Modules:
  0.0 42.3 jit_solution(10344657995304971966)
XLA Ops:
  0.6 0.0 copy-start.1
  0.6 38.0 %attention_block.1 = f32[144,64]{1,0:T(8,128)} custom-call(bf16[144,3,1280]{2,1,0:T(4,128)(2,1)} %bitcast.8, bf16[48,2,640]{2,1,0:T(2,128)(2,1)} %text_hbm.1, f32[1,64]{1,0:T(1,128)} %bitcast.10, f32[1,64]{1,0:T(1,128)} %bitcast.11, f32[1,64]{1,0:T(1,128)} %bitcast.12, bf16[1216,640]{1,0:T(8,128)(2,1)} %bitcast.7, bf16[64,1216]{1,0:T(8,128)(2,1)} %fw_hbm.1, ...), custom_call_target="tpu_custom_call" | custom-call | tf_op jit(solution)/shard_map/attention_block/pallas_call | solution.py:354
  38.6 1.1 %reshape.41 = f32[12,12,2,2,16]{4,3,2,1,0:T(2,128)S(1)} reshape(f32[144,64]{1,0:T(8,128)} %attention_block.1) | data formatting | bytes 73728 | tf_op jit(solution)/shard_map/reshape | solution.py:398
  39.8 0.1 copy.15
  39.9 0.4 reshape.42
  40.2 0.0 copy-start
  41.6 0.0 copy-done.1
  41.7 0.6 %multiply_add_fusion = f32[24,384]{1,0:T(8,128)} fusion(f32[24,384]{1,0:T(8,128)S(1)} %copy-done.1, f32[24,384]{1,0:T(8,128)S(1)} %reshape.42, f32[]{:T(128)} %bitcast.6), kind=kLoop, calls=%fused_computation | loop fusion | flops 18432 | bytes 110596 | tf_op jit(solution)/shard_map/add | solution.py:403
  42.3 0.0 copy-done
Async XLA Ops:
  0.6 41.0 %copy-start.1 = (f32[24,384]{1,0:T(8,128)S(1)}, f32[24,384]{1,0:T(8,128)}, u32[]{:S(2)}) copy-start(f32[24,384]{1,0:T(8,128)} %param.21) | copy-start | bytes 110596
  40.2 2.0 %copy-start = (f32[24,384]{1,0:T(8,128)}, f32[24,384]{1,0:T(8,128)S(1)}, u32[]{:S(2)}) copy-start(f32[24,384]{1,0:T(8,128)S(1)} %reshape.42) | copy-start | bytes 110596

commit v2 on v1

--- a/solution.py
+++ b/solution.py
@@ -20,17 +20,18 @@
 
 
 def noise_level(step_number):
-    fraction = 1.0 - step_number.astype(F32) / STEPS
+    fraction = 1.0 - jnp.full((1, 1), step_number, jnp.int32).astype(F32) / STEPS
     return SHIFT_FACTOR * fraction / (1.0 + (SHIFT_FACTOR - 1.0) * fraction)
 
 
 def block_kernel(
     torus,
-    qkv_hbm, text_hbm, gq_ref, gk_ref, gt_ref, wt_hbm, fw_hbm, hid_hbm, mod_hbm,
-    vel_ref,
-    qkv, text, hid_in, hid, mod, fw, fw_full, gains, block,
+    qkv_hbm, text_hbm, gq_hbm, gk_hbm, gt_hbm, wt_hbm, fw_hbm, hid_hbm, mod_hbm,
+    lat_hbm, index_ref, count_ref,
+    out_ref,
+    qkv, text, hid_in, hid, mod, fw, fw_full, gain_in, gains, block, lat, patch, pixels,
     v_out, k_out, q_out, q_all, k_all, v_all, w_own, w_oth,
-    att_out, att_in, att_own, p_own, p_oth,
+    att_out, att_in, att_own, p_own, p_oth, base,
     load_sem, send_sem, recv_sem, pair_send, pair_recv, w_send, w_recv,
 ):
     row, col = lax.axis_index("row"), lax.axis_index("col")
@@ -60,12 +61,11 @@
     load_fw = load(fw_hbm, fw.at[row], 3)
     load_hid = load(hid_hbm, hid_in, 4)
     load_mod = load(mod_hbm, mod, 5)
+    load_lat = load(lat_hbm, lat, 6)
+    load_gains = [load(ref, gain_in.at[at], 7 + at) for at, ref in enumerate((gq_hbm, gk_hbm, gt_hbm))]
     load_qkv.start()
-    load_text.start()
-    load_w.start()
-    load_fw.start()
-    load_hid.start()
-    load_mod.start()
+    for copy in load_gains:
+        copy.start()
 
     partners = [to_row, to_col]
     if torus:
@@ -80,19 +80,20 @@
 
         to_y = {"req": chip(at_x, at_y + size_y + 2 * col - 1, at_z), "col": 1 - col}
         to_x = [{"req": chip(at_x + step, at_y, at_z)} for step in (1, size_x - 1)]
-        to_z = [{"req": chip(at_x, at_y, at_z + step)} for step in (1, size_z - 1)]
-        partners += [to_y, *to_x, *to_z]
+        partners += [to_y, *to_x]
 
     barrier = pltpu.get_barrier_semaphore()
     for partner in partners:
         pl.semaphore_signal(barrier, inc=1, device_id=partner, device_id_type=MESH)
 
-    for at, ref in enumerate((gq_ref, gk_ref, gt_ref)):
-        gains[at : at + 1, 0:HEAD] = ref[...]
-        gains[at : at + 1, HEAD:LANES] = ref[...]
     down = lax.broadcasted_iota(jnp.int32, (2 * LANES, LANES), 0) // HEAD
     across = lax.broadcasted_iota(jnp.int32, (2 * LANES, LANES), 1) // HEAD
     block[...] = jnp.where(down % 2 == across, 1.0 / HEAD, 0.0).astype(BF16)
+
+    for at, copy in enumerate(load_gains):
+        copy.wait()
+        gains[at : at + 1, 0:HEAD] = gain_in[at]
+        gains[at : at + 1, HEAD:LANES] = gain_in[at]
 
     pl.semaphore_wait(barrier, len(partners))
 
@@ -100,17 +101,17 @@
         quarter = half // 4
         first = quarter // 32 * 16 + 16
         parts = ((0, first), (first, quarter - first))
-        colour = (at_x + 2 * at_z) % 4
 
         def piece(which, part, base):
             start, count = parts[part]
             offset = base + (which % 4) * quarter + start
             return pl.ds(pl.multiple_of(offset, 16), count)
 
-        def near(part):
+        def near(side, part):
+            which = at_x + 2 * side
             return remote(
-                wt_hbm.at[piece(colour, part, 0)],
-                w_oth.at[piece(colour, part, row * half)], weight, part, to_y,
+                wt_hbm.at[piece(which, part, 0)],
+                w_oth.at[piece(which, part, row * half)], weight, 2 * side + part, to_y,
             )
 
         def spread(which, part, at, device):
@@ -118,16 +119,14 @@
             return remote(w_oth.at[rows], w_oth.at[rows], weight, at, device)
 
         def across_x(part, side, which):
-            return spread(which, part, 2 + 2 * side + part, to_x[side])
-
-        def across_z(part, which):
-            return spread(which, part, 6 + part, to_z[part])
-
-        def across_row(which, part, at):
-            return spread(which, part, at, to_row)
-
-        near(0).start()
-        near(1).start()
+            return spread(which, part, 4 + 2 * side + part, to_x[side])
+
+        def across_row(part, away):
+            return spread(at_x + away, part, 8 + 2 * away + part, to_row)
+
+        for side in range(2):
+            for part in range(2):
+                near(side, part).start()
     else:
         near = remote(wt_hbm, w_oth.at[own_half], weight, 0, to_col)
     w_row = remote(wt_hbm, w_own.at[own_half], plain, 0, to_row)
@@ -178,6 +177,8 @@
         return remote(att_out.at[at], att_in.at[at], paired, 5 * pairs + at, to_col)
 
     load_qkv.wait()
+    for copy in (load_text, load_w, load_fw, load_hid, load_mod, load_lat):
+        copy.start()
     for at, part in enumerate(split(qkv[:, 2, other])):
         v_out[at] = part
     v_col(0).start()
@@ -215,11 +216,20 @@
     q_all[:, col_rows, :] = head_norm(qkv[:, 0, mine], gains[0:1] * 0.125)
 
     def spread_near(part):
-        near(part).wait_recv()
-        across_x(part, 0, colour).start()
-        across_x(part, 1, colour).start()
-        across_z(part, colour).start()
-        across_row(colour, part, 8 + part).start()
+        near(0, part).wait_recv()
+        across_x(part, 0, at_x).start()
+        across_x(part, 1, at_x).start()
+        across_row(part, 0).start()
+
+    def pass_x(part):
+        across_x(part, 0, at_x + 3).wait_recv()
+        across_row(part, 3).start()
+        across_x(part, 1, at_x + 1).wait_recv()
+        across_row(part, 1).start()
+
+    def pass_near(part):
+        near(1, part).wait_recv()
+        across_row(part, 2).start()
 
     v_row.wait()
     k_row.wait()
@@ -259,30 +269,27 @@
         k_far(at).start()
         v_col(at).wait_recv()
         v_far(at).start()
+        if torus and at == 1:
+            spread_near(0)
+        if at > 0:
+            attend_pair(at - 1)
         if at == 0:
             load_hid.wait()
             for line in range(hid_in.shape[0]):
                 hid[grid_cols * line : grid_cols * (line + 1), :] = hid_in[line]
-        else:
-            attend_pair(at - 1)
-        if torus and at == 0:
-            spread_near(0)
-        if torus and at == 1:
-            spread_near(1)
-        if torus and at == pairs - 1:
-            for part in range(2):
-                across_x(part, 0, colour + 3).wait_recv()
-                across_row(colour + 3, part, 10 + part).start()
-                across_x(part, 1, colour + 1).wait_recv()
-                across_row(colour + 1, part, 12 + part).start()
-                across_z(part, colour + 2).wait_recv()
-                across_row(colour + 2, part, 14 + part).start()
-        if at == 1:
             load_fw.wait()
             fw_row.wait()
             fw_full[:, 0:half] = fw[0]
             fw_full[:, half:features] = fw[1]
+        if torus and at == 2:
+            spread_near(1)
+        if torus and at == 3:
+            pass_x(0)
+        if torus and at == 4:
+            pass_near(0)
     attend_pair(pairs - 1)
+    if torus:
+        pass_x(1)
 
     def project(attended, weights):
         joined = jnp.concatenate([attended[at] for at in range(pairs)], axis=1)
@@ -290,15 +297,22 @@
             joined, weights[...], (((1,), (1,)), ((), ())), preferred_element_type=F32
         ).astype(BF16)
 
+    rows = tile // 3
     load_w.wait()
     w_row.wait()
+    load_mod.wait()
     p_own[...] = project(att_own, w_own)
+
+    @pl.loop(0, 3)
+    def _(at):
+        part = pl.ds(pl.multiple_of(at * rows, 16), rows)
+        base[part, :] = hid[part, :].astype(F32) + mod[2:3, :] * p_own[part, :].astype(F32)
+
     if torus:
+        pass_near(1)
         for part in range(2):
-            across_row(colour, part, 8 + part).wait()
-            across_row(colour + 3, part, 10 + part).wait()
-            across_row(colour + 1, part, 12 + part).wait()
-            across_row(colour + 2, part, 14 + part).wait()
+            for away in range(4):
+                across_row(part, away).wait()
     else:
         near.wait()
         w_far = remote(w_oth.at[own_half], w_oth.at[own_half], weight, 1, to_row)
@@ -307,33 +321,50 @@
     for at in range(pairs):
         att_col(at).wait_recv()
     p_oth[...] = project(att_in, w_oth)
-    load_mod.wait()
-
-    rows = tile // 3
 
     @pl.loop(0, 3)
     def _(at):
         part = pl.ds(pl.multiple_of(at * rows, 16), rows)
-        projected = p_own[part, :].astype(F32) + p_oth[part, :].astype(F32)
-        mixed = hid[part, :].astype(F32) + mod[2:3, :] * projected
+        mixed = base[part, :] + mod[2:3, :] * p_oth[part, :].astype(F32)
         mean = jnp.sum(mixed, axis=-1, keepdims=True) * (1.0 / features)
         centered = mixed - mean
         var = jnp.sum(centered * centered, axis=-1, keepdims=True) * (1.0 / features)
         normed = centered * lax.rsqrt(var + EPS) * (1.0 + mod[1:2, :]) + mod[0:1, :]
-        vel_ref[part, :] = lax.dot_general(
+        patch[part, 0:HEAD] = lax.dot_general(
             normed.astype(BF16), fw_full[...], (((1,), (1,)), ((), ())),
             preferred_element_type=F32,
         )
+
+    load_lat.wait()
+    span = PATCH * CH
+    side = tile // grid_cols
+    lane = lax.broadcasted_iota(jnp.int32, (side, LANES), 1) // span
+    euler = noise_level(index_ref[0] + count_ref[0]) - noise_level(index_ref[0])
+    step = LANES // span
+    for first_col in range(0, grid_cols, step):
+        columns = [
+            patch[pl.ds(first_col + at, side, stride=grid_cols), :] for at in range(step)
+        ]
+        lanes = slice(first_col * span, (first_col + step) * span)
+        for line in range(PATCH):
+            merged = jnp.zeros((side, LANES), F32)
+            for at, values in enumerate(columns):
+                moved = pltpu.roll(values, (at - line) % step * span, 1)
+                merged = jnp.where(lane == at, moved, merged)
+            pixels[first_col // step, pl.ds(line, side, stride=PATCH), :] = merged
+        velocity = pixels[first_col // step]
+        out_ref[0, :, lanes] = velocity
+        out_ref[1, :, lanes] = lat[:, lanes] + euler * velocity
 
     for at in range(pairs):
         for copy in (k_col, v_col, q_col, k_far, v_far, att_col):
             copy(at).wait_send()
     if torus:
         for part in range(2):
-            near(part).wait_send()
-            across_x(part, 0, colour).wait_send()
-            across_x(part, 1, colour).wait_send()
-            across_z(part, colour).wait_send()
+            near(0, part).wait_send()
+            near(1, part).wait_send()
+            across_x(part, 0, at_x).wait_send()
+            across_x(part, 1, at_x).wait_send()
 
 
 def on_device(
@@ -349,12 +380,12 @@
     patch_values = final_weight.shape[0]
     keys = 4 * tile + 2 * words
     pairs = width // LANES
-    anywhere = pl.BlockSpec(memory_space=pl.ANY)
+    anywhere = pl.BlockSpec(memory_space=pltpu.HBM)
     vmem = pl.BlockSpec(memory_space=pltpu.VMEM)
-    velocity = pl.pallas_call(
+    both = pl.pallas_call(
         functools.partial(block_kernel, torus),
-        out_shape=jax.ShapeDtypeStruct((tile, patch_values), F32),
-        in_specs=[anywhere, anywhere, vmem, vmem, vmem, anywhere, anywhere, anywhere, anywhere],
+        out_shape=jax.ShapeDtypeStruct((2, *latent.shape), F32),
+        in_specs=[anywhere] * 10 + [pl.BlockSpec(memory_space=pltpu.SMEM)] * 2,
         out_specs=vmem,
         scratch_shapes=[
             pltpu.VMEM((tile, 3, heads_width), BF16),
@@ -364,8 +395,12 @@
             pltpu.VMEM((3, features), F32),
             pltpu.VMEM((2, patch_values, half), BF16),
             pltpu.VMEM((patch_values, features), BF16),
+            pltpu.VMEM((3, 1, HEAD), F32),
             pltpu.VMEM((8, LANES), F32),
             pltpu.VMEM((2 * LANES, LANES), BF16),
+            pltpu.VMEM(latent.shape, F32),
+            pltpu.VMEM((tile, LANES), F32),
+            pltpu.VMEM((latent.shape[1] // LANES, latent.shape[0], LANES), F32),
             pltpu.VMEM((pairs, tile, LANES), BF16),
             pltpu.VMEM((pairs, tile, LANES), BF16),
             pltpu.VMEM((pairs, tile, LANES), BF16),
@@ -379,7 +414,8 @@
             pltpu.VMEM((pairs, tile, LANES), BF16),
             pltpu.VMEM((tile, features), BF16),
             pltpu.VMEM((tile, features), BF16),
-            pltpu.SemaphoreType.DMA((6,)),
+            pltpu.VMEM((tile, features), F32),
+            pltpu.SemaphoreType.DMA((10,)),
             pltpu.SemaphoreType.DMA((6,)),
             pltpu.SemaphoreType.DMA((6,)),
             pltpu.SemaphoreType.DMA((6 * pairs,)),
@@ -387,20 +423,23 @@
             pltpu.SemaphoreType.DMA((16,)),
             pltpu.SemaphoreType.DMA((16,)),
         ],
-        compiler_params=pltpu.CompilerParams(collective_id=0, has_side_effects=True),
+        compiler_params=pltpu.CompilerParams(
+            collective_id=0, has_side_effects=True, vmem_limit_bytes=40 * 1024 * 1024
+        ),
         name="attention_block",
     )(
-        image_qkv.reshape(tile, 3, heads_width), text_kv,
-        gain_query.reshape(1, HEAD), gain_key.reshape(1, HEAD), gain_text.reshape(1, HEAD),
-        out_weight.T, final_weight, hidden, modulation,
+        *(
+            pltpu.with_memory_space_constraint(operand, pltpu.HBM)
+            for operand in (
+                image_qkv.reshape(tile, 3, heads_width), text_kv,
+                gain_query.reshape(1, HEAD), gain_key.reshape(1, HEAD),
+                gain_text.reshape(1, HEAD), out_weight.T, final_weight, hidden, modulation,
+                latent,
+            )
+        ),
+        step_index, step_count,
     )
-    velocity = (
-        velocity.reshape(tile_rows, tile_cols, PATCH, PATCH, CH)
-        .transpose(0, 2, 1, 3, 4)
-        .reshape(tile_rows * PATCH, tile_cols * PATCH * CH)
-    )
-    euler_step = noise_level(step_index[0] + step_count[0]) - noise_level(step_index[0])
-    return (velocity, latent + euler_step * velocity)
+    return (both[0], both[1])
 
 
 def solution(mesh):

time: 42.9 us -> 37.1 us (0.86); the launches traced: 42.3 us -> 36.9 us
  Pallas kernels: 38 us -> 34.4 us
  local copies, waits for them, and re-layouts: 1.62 us -> 0.63 us
  other arithmetic: 0.62 us -> 0 us
    pallas_call x1, Pallas kernels: 38 us -> 34.4 us  [on_device(): pl.pallas_call(functools.partial(block_kernel, torus), out_shape=jax.Shap...]
    reshape x2 -> x0, local copies, waits for them, and re-layouts: 1.51 us -> none  [the longest x1 1.15 us: on_device(): velocity.reshape(tile_rows, tile_cols, PATCH, PATCH, CH)]
    squeeze x0 -> x1, local copies, waits for them, and re-layouts: none -> 0.63 us  [on_device(): return (both[0], both[1])]
    add x1 -> x0, other arithmetic: 0.62 us -> none  [on_device(): return (velocity, latent + euler_step * velocity)]
where the time goes in v2:
time: 37.1 us; the launch traced here: 36.9 us
  Pallas kernels  34.4 us (93%)
  between operations  1.93 us (5%)
  local copies, waits for them, and re-layouts  0.63 us (2%)
    pallas_call x1, Pallas kernels, on_device(): pl.pallas_call(functools.partial(block_kernel, torus), out_shape=jax.Shap...  34.4 us

profile of v2, /device:TPU:1, one launch (start us, length us, event | category | flops | bytes accessed | tf_op | source)
XLA Modules:
  0.0 36.9 jit_solution(959446726993016848)
XLA Ops:
  1.9 34.4 %attention_block.1 = f32[2,24,384]{2,1,0:T(8,128)S(1)} custom-call(bf16[144,3,1280]{2,1,0:T(4,128)(2,1)} %bitcast.10, bf16[48,2,640]{2,1,0:T(2,128)(2,1)} %text_hbm.1, f32[1,64]{1,0:T(1,128)} %bitcast.11, f32[1,64]{1,0:T(1,128)} %bitcast.12, f32[1,64]{1,0:T(1,128)} %bitcast.13, bf16[1216,640]{1,0:T(8,128)(2,1)} %bitcast.9, bf16[64,1216]{1,0:T(8,128)(2,1)} %fw_hbm.1, ...), custom_call_target="tpu_custom_call" | custom-call | tf_op jit(solution)/shard_map/attention_block/pallas_call | solution.py:385
  36.3 0.6 %slice_bitcast_fusion = (f32[24,384]{1,0:T(8,128)}, f32[24,384]{1,0:T(8,128)}) fusion(f32[2,24,384]{2,1,0:T(8,128)S(1)} %attention_block.1), kind=kLoop, calls=%fused_computation | loop fusion | bytes 147456 | tf_op jit(solution)/shard_map/squeeze | solution.py:442

commit v3 on v2

--- a/solution.py
+++ b/solution.py
@@ -31,7 +31,7 @@
     out_ref,
     qkv, text, hid_in, hid, mod, fw, fw_full, gain_in, gains, block, lat, patch, pixels,
     v_out, k_out, q_out, q_all, k_all, v_all, w_own, w_oth,
-    att_out, att_in, att_own, p_own, p_oth, base,
+    att_out, att_in, att_own, p_oth, base,
     load_sem, send_sem, recv_sem, pair_send, pair_recv, w_send, w_recv,
 ):
     row, col = lax.axis_index("row"), lax.axis_index("col")
@@ -99,8 +99,8 @@
 
     if torus:
         quarter = half // 4
-        first = quarter // 32 * 16 + 16
-        parts = ((0, first), (first, quarter - first))
+        third = quarter // 48 * 16
+        parts = ((0, third), (third, quarter - 2 * third), (quarter - third, third))
 
         def piece(which, part, base):
             start, count = parts[part]
@@ -119,18 +119,24 @@
             return remote(w_oth.at[rows], w_oth.at[rows], weight, at, device)
 
         def across_x(part, side, which):
-            return spread(which, part, 4 + 2 * side + part, to_x[side])
+            return spread(which, part, 5 + 3 * side + part, to_x[side])
+
+        def across_two(which):
+            return spread(which, 0, 11, to_x[0])
 
         def across_row(part, away):
-            return spread(at_x + away, part, 8 + 2 * away + part, to_row)
-
-        for side in range(2):
-            for part in range(2):
-                near(side, part).start()
+            return spread(at_x + away, part, 12 + 3 * away + part, to_row)
+
+        for part in range(3):
+            near(0, part).start()
+        near(1, 1).start()
+        near(1, 2).start()
     else:
         near = remote(wt_hbm, w_oth.at[own_half], weight, 0, to_col)
     w_row = remote(wt_hbm, w_own.at[own_half], plain, 0, to_row)
     fw_row = remote(fw_hbm, fw.at[row], plain, 1, to_row)
+    w_row.start()
+    fw_row.start()
 
     def head_norm(values, gain):
         count = values.shape[0]
@@ -209,8 +215,6 @@
     k_all[:, own_text, :] = head_norm(text[:, 0, :], gains[2:3])
     kt_row = remote(k_all.at[:, own_text], k_all.at[:, row_text], plain, 5, to_row)
     kt_row.start()
-    w_row.start()
-    fw_row.start()
     if not torus:
         near.start()
     q_all[:, col_rows, :] = head_norm(qkv[:, 0, mine], gains[0:1] * 0.125)
@@ -223,6 +227,8 @@
 
     def pass_x(part):
         across_x(part, 0, at_x + 3).wait_recv()
+        if part == 0:
+            across_two(at_x + 3).start()
         across_row(part, 3).start()
         across_x(part, 1, at_x + 1).wait_recv()
         across_row(part, 1).start()
@@ -263,14 +269,23 @@
         att_col(at).start()
         att_own[at] = attend(at, col_rows)
 
+    def project(attended, weights, first, last):
+        joined = jnp.concatenate([attended[at] for at in range(first, last)], axis=1)
+        return lax.dot_general(
+            joined, weights[:, LANES * first : LANES * last], (((1,), (1,)), ((), ())),
+            preferred_element_type=F32,
+        )
+
     grid_cols = hid_in.shape[1]
     for at in range(pairs):
         k_col(at).wait_recv()
         k_far(at).start()
         v_col(at).wait_recv()
         v_far(at).start()
-        if torus and at == 1:
-            spread_near(0)
+        if torus and at < 2:
+            spread_near(at)
+        if torus and at == 3:
+            pass_x(0)
         if at > 0:
             attend_pair(at - 1)
         if at == 0:
@@ -282,35 +297,34 @@
             fw_full[:, 0:half] = fw[0]
             fw_full[:, half:features] = fw[1]
         if torus and at == 2:
-            spread_near(1)
+            spread_near(2)
         if torus and at == 3:
-            pass_x(0)
+            pass_x(1)
         if torus and at == 4:
-            pass_near(0)
+            pass_near(1)
+        if at == 3:
+            load_w.wait()
+            w_row.wait()
+            base[...] = project(att_own, w_own, 0, 2)
     attend_pair(pairs - 1)
     if torus:
-        pass_x(1)
-
-    def project(attended, weights):
-        joined = jnp.concatenate([attended[at] for at in range(pairs)], axis=1)
-        return lax.dot_general(
-            joined, weights[...], (((1,), (1,)), ((), ())), preferred_element_type=F32
-        ).astype(BF16)
+        pass_x(2)
+        pass_near(2)
 
     rows = tile // 3
-    load_w.wait()
-    w_row.wait()
     load_mod.wait()
-    p_own[...] = project(att_own, w_own)
+    base[...] += project(att_own, w_own, 2, pairs)
 
     @pl.loop(0, 3)
     def _(at):
         part = pl.ds(pl.multiple_of(at * rows, 16), rows)
-        base[part, :] = hid[part, :].astype(F32) + mod[2:3, :] * p_own[part, :].astype(F32)
+        product = base[part, :].astype(BF16).astype(F32)
+        base[part, :] = hid[part, :].astype(F32) + mod[2:3, :] * product
 
     if torus:
-        pass_near(1)
-        for part in range(2):
+        across_two(at_x + 2).wait_recv()
+        across_row(0, 2).start()
+        for part in range(3):
             for away in range(4):
                 across_row(part, away).wait()
     else:
@@ -320,7 +334,7 @@
         w_far.wait()
     for at in range(pairs):
         att_col(at).wait_recv()
-    p_oth[...] = project(att_in, w_oth)
+    p_oth[...] = project(att_in, w_oth, 0, pairs).astype(BF16)
 
     @pl.loop(0, 3)
     def _(at):
@@ -330,10 +344,11 @@
         centered = mixed - mean
         var = jnp.sum(centered * centered, axis=-1, keepdims=True) * (1.0 / features)
         normed = centered * lax.rsqrt(var + EPS) * (1.0 + mod[1:2, :]) + mod[0:1, :]
-        patch[part, 0:HEAD] = lax.dot_general(
-            normed.astype(BF16), fw_full[...], (((1,), (1,)), ((), ())),
-            preferred_element_type=F32,
-        )
+        p_oth[part, :] = normed.astype(BF16)
+
+    patch[:, 0:HEAD] = lax.dot_general(
+        p_oth[...], fw_full[...], (((1,), (1,)), ((), ())), preferred_element_type=F32
+    )
 
     load_lat.wait()
     span = PATCH * CH
@@ -360,9 +375,11 @@
         for copy in (k_col, v_col, q_col, k_far, v_far, att_col):
             copy(at).wait_send()
     if torus:
-        for part in range(2):
+        across_two(at_x + 3).wait_send()
+        near(1, 1).wait_send()
+        near(1, 2).wait_send()
+        for part in range(3):
             near(0, part).wait_send()
-            near(1, part).wait_send()
             across_x(part, 0, at_x).wait_send()
             across_x(part, 1, at_x).wait_send()
 
@@ -413,15 +430,14 @@
             pltpu.VMEM((pairs, tile, LANES), BF16),
             pltpu.VMEM((pairs, tile, LANES), BF16),
             pltpu.VMEM((tile, features), BF16),
-            pltpu.VMEM((tile, features), BF16),
             pltpu.VMEM((tile, features), F32),
             pltpu.SemaphoreType.DMA((10,)),
             pltpu.SemaphoreType.DMA((6,)),
             pltpu.SemaphoreType.DMA((6,)),
             pltpu.SemaphoreType.DMA((6 * pairs,)),
             pltpu.SemaphoreType.DMA((6 * pairs,)),
-            pltpu.SemaphoreType.DMA((16,)),
-            pltpu.SemaphoreType.DMA((16,)),
+            pltpu.SemaphoreType.DMA((24,)),
+            pltpu.SemaphoreType.DMA((24,)),
         ],
         compiler_params=pltpu.CompilerParams(
             collective_id=0, has_side_effects=True, vmem_limit_bytes=40 * 1024 * 1024

time: 37.1 us -> 35.6 us (0.960)
  Pallas kernels: 34.4 us -> 32.9 us
    pallas_call x1, Pallas kernels: 34.4 us -> 32.9 us  [on_device(): pl.pallas_call(functools.partial(block_kernel, torus), out_shape=jax.Shap...]
where the time goes in v3:
time: 35.6 us; the launch traced here: 35.4 us
  Pallas kernels  32.9 us (92%)
  between operations  1.93 us (5%)
  local copies, waits for them, and re-layouts  0.63 us (2%)
    pallas_call x1, Pallas kernels, on_device(): pl.pallas_call(functools.partial(block_kernel, torus), out_shape=jax.Shap...  32.9 us

profile of v3, /device:TPU:1, one launch (start us, length us, event | category | flops | bytes accessed | tf_op | source)
XLA Modules:
  0.0 35.4 jit_solution(13818457172303407141)
XLA Ops:
  1.9 32.9 %attention_block.1 = f32[2,24,384]{2,1,0:T(8,128)S(1)} custom-call(bf16[144,3,1280]{2,1,0:T(4,128)(2,1)} %bitcast.10, bf16[48,2,640]{2,1,0:T(2,128)(2,1)} %text_hbm.1, f32[1,64]{1,0:T(1,128)} %bitcast.11, f32[1,64]{1,0:T(1,128)} %bitcast.12, f32[1,64]{1,0:T(1,128)} %bitcast.13, bf16[1216,640]{1,0:T(8,128)(2,1)} %bitcast.9, bf16[64,1216]{1,0:T(8,128)(2,1)} %fw_hbm.1, ...), custom_call_target="tpu_custom_call" | custom-call | tf_op jit(solution)/shard_map/attention_block/pallas_call | solution.py:402
  34.8 0.6 %slice_bitcast_fusion = (f32[24,384]{1,0:T(8,128)}, f32[24,384]{1,0:T(8,128)}) fusion(f32[2,24,384]{2,1,0:T(8,128)S(1)} %attention_block.1), kind=kLoop, calls=%fused_computation | loop fusion | bytes 147456 | tf_op jit(solution)/shard_map/squeeze | solution.py:458

commit v4 on v3

--- a/solution.py
+++ b/solution.py
@@ -90,11 +90,6 @@
     across = lax.broadcasted_iota(jnp.int32, (2 * LANES, LANES), 1) // HEAD
     block[...] = jnp.where(down % 2 == across, 1.0 / HEAD, 0.0).astype(BF16)
 
-    for at, copy in enumerate(load_gains):
-        copy.wait()
-        gains[at : at + 1, 0:HEAD] = gain_in[at]
-        gains[at : at + 1, HEAD:LANES] = gain_in[at]
-
     pl.semaphore_wait(barrier, len(partners))
 
     if torus:
@@ -189,6 +184,10 @@
         v_out[at] = part
     v_col(0).start()
     v_col(1).start()
+    for at, copy in enumerate(load_gains):
+        copy.wait()
+        gains[at : at + 1, 0:HEAD] = gain_in[at]
+        gains[at : at + 1, HEAD:LANES] = gain_in[at]
     k_out[...] = head_norm(qkv[:, 1, other], gains[1:2])
     k_col(0).start()
     q_out[...] = head_norm(qkv[:, 0, other], gains[0:1] * 0.125)

time: 35.6 us -> 35.5 us (level)
  no operation moved by 1% of the time
where the time goes in v4:
time: 35.5 us; the launch traced here: 35.3 us
  Pallas kernels  32.8 us (92%)
  between operations  1.93 us (5%)
  local copies, waits for them, and re-layouts  0.63 us (2%)
    pallas_call x1, Pallas kernels, on_device(): pl.pallas_call(functools.partial(block_kernel, torus), out_shape=jax.Shap...  32.8 us

profile of v4, /device:TPU:1, one launch (start us, length us, event | category | flops | bytes accessed | tf_op | source)
XLA Modules:
  0.0 35.3 jit_solution(3303326989450094508)
XLA Ops:
  1.9 32.8 %attention_block.1 = f32[2,24,384]{2,1,0:T(8,128)S(1)} custom-call(bf16[144,3,1280]{2,1,0:T(4,128)(2,1)} %bitcast.10, bf16[48,2,640]{2,1,0:T(2,128)(2,1)} %text_hbm.1, f32[1,64]{1,0:T(1,128)} %bitcast.11, f32[1,64]{1,0:T(1,128)} %bitcast.12, f32[1,64]{1,0:T(1,128)} %bitcast.13, bf16[1216,640]{1,0:T(8,128)(2,1)} %bitcast.9, bf16[64,1216]{1,0:T(8,128)(2,1)} %fw_hbm.1, ...), custom_call_target="tpu_custom_call" | custom-call | tf_op jit(solution)/shard_map/attention_block/pallas_call | solution.py:401
  34.7 0.6 %slice_bitcast_fusion = (f32[24,384]{1,0:T(8,128)}, f32[24,384]{1,0:T(8,128)}) fusion(f32[2,24,384]{2,1,0:T(8,128)S(1)} %attention_block.1), kind=kLoop, calls=%fused_computation | loop fusion | bytes 147456 | tf_op jit(solution)/shard_map/squeeze | solution.py:457
